TPU v7x, 512 devices: a whole 4x8x8 slice. The times are simulated.
512 devices in a mesh: row: 16 (over y_hi, x), col: 32 (over z, y_lo, core).
Axes of the slice: x: 4, y: 8 (y_hi: 4, y_lo: 2; y = y_hi * 2 + y_lo), z: 8, core: 2. Of those that a mesh axis runs over, the one named last changes fastest.
Arguments:
- query: bfloat16 [16384, 1024], P(('row', 'col')), may hold values from -0.5375 to 0.5375
- passage: bfloat16 [16384, 1024], P(('row', 'col')), may hold values from -0.43 to 0.43
- positive: int32 [512, 32], P(('row', 'col')), may hold values from 0 to 31, each once within a row
Outputs:
- loss_value: float32 [], replicated
- grad_query: bfloat16 [16384, 1024], P(('row', 'col'))
- grad_passage: bfloat16 [16384, 1024], P(('row', 'col'))
Inputs may be any that keep to these rules, and one draw needn't show every extreme that they name: Each row of positive names every position 0 to 31 once.
All inputs are finite; a program needn't handle non-finite values.
Results may differ from a plain program's by a relative error of at most 0.015.
Values may be sent and summed in bfloat16 or wider, within the bound.
No kernel may reach another device: no remote copies, remote signals or barrier semaphores. Data moves between devices by JAX's collectives and lax.ppermute only.
A program may use at most 64 MiB of HBM per device.

v0:
```python
import jax
import jax.numpy as jnp
from jax import lax
from jax.sharding import PartitionSpec as P

logit_scale = 20.0


def tile_scores(query_rows, passage_rows):
    return logit_scale * lax.dot_general(
        query_rows, passage_rows, (((1,), (1,)), ((), ())), preferred_element_type=jnp.float32
    )


def local(query, passage, positive):
    shard_rows = query.shape[0]
    row_devices = lax.axis_size("row")
    col_devices = lax.axis_size("col")
    passage_all = lax.all_gather(passage, "row", axis=0, tiled=True)
    query_all = lax.all_gather(query, "col", axis=0, tiled=True)
    scores = tile_scores(query_all, passage_all)
    row_local_peak = scores.max(axis=1)
    col_local_peak = scores.max(axis=0)
    row_peak = lax.pmax(row_local_peak, "col")
    col_peak = lax.pmax(col_local_peak, "row")
    row_sum = lax.psum(jnp.exp(scores - row_peak[:, None]).sum(axis=1), "col")
    col_sum = lax.psum(jnp.exp(scores - col_peak[None, :]).sum(axis=0), "row")
    row_lse = row_peak + jnp.log(row_sum)
    col_lse = col_peak + jnp.log(col_sum)
    weights = (
        0.5 * (jnp.exp(scores - row_lse[:, None]) + jnp.exp(scores - col_lse[None, :]))
    ).astype(jnp.bfloat16)
    query_sum = lax.psum_scatter(
        jnp.dot(weights, passage_all, preferred_element_type=jnp.float32).astype(jnp.bfloat16),
        "col",
        scatter_dimension=0,
        tiled=True,
    ).astype(jnp.float32)
    passage_sum = lax.psum_scatter(
        lax.dot_general(
            weights, query_all, (((0,), (0,)), ((), ())), preferred_element_type=jnp.float32
        ).astype(jnp.bfloat16),
        "row",
        scatter_dimension=0,
        tiled=True,
    ).astype(jnp.float32)
    slot_index = jnp.arange(shard_rows, dtype=jnp.int32)
    onehot = (positive[0][:, None] == slot_index[None, :]).astype(jnp.bfloat16)
    paired_passage = jnp.dot(onehot, passage, preferred_element_type=jnp.float32)
    paired_query = lax.dot_general(
        onehot, query, (((0,), (0,)), ((), ())), preferred_element_type=jnp.float32
    )
    positive_score = logit_scale * jnp.sum(query.astype(jnp.float32) * paired_passage, axis=1)
    grad_query = (logit_scale * (query_sum - paired_passage)).astype(jnp.bfloat16)
    grad_passage = (logit_scale * (passage_sum - paired_query)).astype(jnp.bfloat16)
    row_part = lax.dynamic_slice_in_dim(row_lse, lax.axis_index("col") * shard_rows, shard_rows)
    col_part = lax.dynamic_slice_in_dim(col_lse, lax.axis_index("row") * shard_rows, shard_rows)
    local_terms = jnp.sum(row_part) + jnp.sum(col_part) - 2.0 * jnp.sum(positive_score)
    summed = lax.psum(local_terms, ("row", "col"))
    loss_value = summed / (2.0 * shard_rows * row_devices * col_devices)
    return (loss_value, grad_query, grad_passage)


def solution(mesh):
    return jax.shard_map(
        local,
        mesh=mesh,
        in_specs=(P(("row", "col"), None), P(("row", "col"), None), P(("row", "col"), None)),
        out_specs=(P(), P(("row", "col"), None), P(("row", "col"), None)),
        check_vma=False,
    )
```

profile of v0, /device:TPU:1, one launch (start us, length us, event | category | flops | bytes accessed | tf_op | source)
XLA Modules:
  0.0 658.9 jit_solution(3152972070807338193)
XLA Ops:
  7.2 0.0 all-gather.5.cloned.1.call-start
  7.2 0.7 all-gather.5.cloned.1.call-update
  7.9 0.0 all-gather.3.cloned.1.call-start
  7.9 0.7 all-gather.3.cloned.1.call-update
  8.6 0.0 reduce-scatter.3.cloned.1.call-start
  8.7 64.2 %all-gather.5.cloned.1.call-done = bf16[512,1024]{1,0:T(8,128)(2,1)} async-done(((bf16[32,1024]{1,0:T(8,128)(2,1)}), bf16[512,1024]{1,0:T(8,128)(2,1)}) %all-gather.5.cloned.1.call-update) | async-done | bytes 1048592 | tf_op jit(solution)/shard_map/all_gather | solution.py:19
  72.9 69.4 %all-gather.3.cloned.1.call-done = bf16[1024,1024]{1,0:T(8,128)(2,1)} async-done(((bf16[32,1024]{1,0:T(8,128)(2,1)}), bf16[1024,1024]{1,0:T(8,128)(2,1)}) %all-gather.3.cloned.1.call-update) | async-done | bytes 2097168 | tf_op jit(solution)/shard_map/all_gather | solution.py:20
  142.3 3.2 fusion.5
  145.5 0.0 copy-start.3
  145.5 37.5 %pmax.15 = f32[512]{0:T(512)S(1)} all-reduce(f32[512]{0:T(512)S(1)} %get-tuple-element.5), channel_id=1, replica_groups=mesh['row'=16,'col'=32] {'row'}, use_global_device_ids=true, to_apply=%region_6.0 | all-reduce | flops 512 | bytes 4096 | tf_op jit(solution)/shard_map/pmax | solution.py:25
  183.0 59.6 %pmax.14 = f32[1024]{0:T(1024)S(1)} all-reduce(f32[1024]{0:T(1024)S(1)} %get-tuple-element.6), channel_id=1, replica_groups=mesh['row'=16,'col'=32] {'col'}, use_global_device_ids=true, to_apply=%region_1.0 | all-reduce | flops 1024 | bytes 8192 | tf_op jit(solution)/shard_map/pmax | solution.py:24
  242.6 1.0 exponential_reduce_fusion
  243.5 32.1 %psum.22 = f32[512]{0:T(512)S(1)} all-reduce(f32[512]{0:T(512)S(1)} %get-tuple-element.3), channel_id=1, replica_groups=mesh['row'=16,'col'=32] {'row'}, use_global_device_ids=true, to_apply=%region_8.0 | all-reduce | flops 512 | bytes 4096 | tf_op jit(solution)/shard_map/psum | solution.py:27
  275.7 59.9 %psum.21 = f32[1024]{0:T(1024)S(1)} all-reduce(f32[1024]{0:T(1024)S(1)} %get-tuple-element.4), channel_id=1, replica_groups=mesh['row'=16,'col'=32] {'col'}, use_global_device_ids=true, to_apply=%region_3.0 | all-reduce | flops 1024 | bytes 8192 | tf_op jit(solution)/shard_map/psum | solution.py:26
  335.6 0.0 copy-done.3
  335.6 2.9 convolution_convert_fusion
  338.5 0.0 reduce-scatter.3.cloned.1.call-update
  338.5 0.0 copy-start
  338.5 0.0 copy-start.1
  338.5 0.0 copy-start.2
  338.5 0.0 reduce-scatter.5.cloned.1.call-start
  338.6 4.0 convolution_convert_fusion.1
  342.6 0.0 reduce-scatter.5.cloned.1.call-update
  342.6 0.7 dynamic-slice_reduce_fusion
  343.3 0.7 dynamic-slice_reduce_fusion.1
  345.3 109.5 %reduce-scatter.3.cloned.1.call-done = bf16[32,1024]{1,0:T(8,128)(2,1)} async-done(((bf16[1024,1024]{1,0:T(8,128)(2,1)}), bf16[32,1024]{1,0:T(8,128)(2,1)}) %reduce-scatter.3.cloned.1.call-update) | async-done | bytes 65552 | tf_op jit(solution)/shard_map/reduce_scatter | solution.py:33
  454.8 0.0 copy-done
  454.8 0.0 copy-done.1
  454.8 0.0 copy-done.2
  454.8 1.8 multiply_convert_fusion.1
  456.6 0.6 multiply_reduce_fusion.1
  457.8 92.4 %reduce-scatter.5.cloned.1.call-done = bf16[32,1024]{1,0:T(8,128)(2,1)} async-done(((bf16[512,1024]{1,0:T(8,128)(2,1)}), bf16[32,1024]{1,0:T(8,128)(2,1)}) %reduce-scatter.5.cloned.1.call-update) | async-done | bytes 65552 | tf_op jit(solution)/shard_map/reduce_scatter | solution.py:39
  550.2 1.7 fusion.1
  551.9 98.7 %psum.23 = f32[]{:T(128)} all-reduce(f32[]{:T(128)S(6)} %sub.45), channel_id=1, replica_groups=mesh['row'=16,'col'=32] {'row','col'}, use_global_device_ids=true, to_apply=%region_12.0 | all-reduce | flops 1 | bytes 8 | tf_op jit(solution)/shard_map/psum | solution.py:59
  (2 shorter events, 0.0 us)
Async XLA Ops:
  7.2 65.8 %all-gather.5.cloned.1.call-start = ((), (), s32[]{:S(2)}) async-start(), calls=%async_computation.3 | async-start | bytes 1114112 | tf_op jit(solution)/shard_map/all_gather | solution.py:19
  7.9 134.4 %all-gather.3.cloned.1.call-start = ((), (), s32[]{:S(2)}) async-start(), calls=%async_computation.2 | async-start | bytes 2162688 | tf_op jit(solution)/shard_map/all_gather | solution.py:20
  8.6 446.1 %reduce-scatter.3.cloned.1.call-start = ((), (), s32[]{:S(2)}) async-start(), calls=%async_computation.4 | async-start | bytes 2162688 | tf_op jit(solution)/shard_map/reduce_scatter | solution.py:33
  145.5 190.1 %copy-start.3 = (bf16[512,1024]{1,0:T(8,128)(2,1)S(1)}, bf16[512,1024]{1,0:T(8,128)(2,1)}, u32[]{:S(2)}) copy-start(bf16[512,1024]{1,0:T(8,128)(2,1)} %all-gather.5.cloned.1.call-done) | copy-start | bytes 3145732
  338.5 116.3 %copy-start = (bf16[32,1024]{1,0:T(8,128)(2,1)S(1)}, bf16[32,1024]{1,0:T(8,128)(2,1)}, u32[]{:S(2)}) copy-start(bf16[32,1024]{1,0:T(8,128)(2,1)} %param.3) | copy-start | bytes 196612
  338.5 116.3 %copy-start.1 = (bf16[32,1024]{1,0:T(8,128)(2,1)S(1)}, bf16[32,1024]{1,0:T(8,128)(2,1)}, u32[]{:S(2)}) copy-start(bf16[32,1024]{1,0:T(8,128)(2,1)} %param.4) | copy-start | bytes 196612
  338.5 116.2 %copy-start.2 = (s32[1,32]{1,0:T(1,128)S(1)}, s32[1,32]{1,0:T(1,128)}, u32[]{:S(2)}) copy-start(s32[1,32]{1,0:T(1,128)} %param.5) | copy-start | bytes 388
  338.5 211.7 %reduce-scatter.5.cloned.1.call-start = ((), (), s32[]{:S(2)}) async-start(), calls=%async_computation.5 | async-start | bytes 1114112 | tf_op jit(solution)/shard_map/reduce_scatter | solution.py:39
Sparse Core Ops, SparseCore 0:
  11.0 61.9 all-gather.4
  75.1 67.1 all-gather.2
  338.6 116.0 reduce-scatter.2
  458.7 91.4 reduce-scatter.4
where the time goes:
time: 659 us
  waiting for transfers between devices  337 us (51%)
  blocking collectives  288 us (44%)
  between operations  17.5 us (3%)
  matrix products  13.7 us (2%)
    reduce_scatter x1, waiting for transfers between devices, local(): lax.psum_scatter(jnp.dot(weights, passage_all, preferred_element_type=jnp...  109 us
    psum x1, blocking collectives, local(): summed = lax.psum(local_terms, ('row', 'col'))  98.7 us
    reduce_scatter x1, waiting for transfers between devices, local(): lax.psum_scatter(lax.dot_general(weights, query_all, (((0,), (0,)), ((),...  92.4 us
    all_gather x1, waiting for transfers between devices, local(): query_all = lax.all_gather(query, 'col', axis=0, tiled=True)  69.4 us
    all_gather x1, waiting for transfers between devices, local(): passage_all = lax.all_gather(passage, 'row', axis=0, tiled=True)  64.2 us
    psum x1, blocking collectives, local(): row_sum = lax.psum(jnp.exp(scores - row_peak[:, None]).sum(axis=1), 'col')  59.9 us
    pmax x1, blocking collectives, local(): row_peak = lax.pmax(row_local_peak, 'col')  59.6 us
    pmax x1, blocking collectives, local(): col_peak = lax.pmax(col_local_peak, 'row')  37.5 us
  transfers between devices with their start and end apart: 4, of which 4 were waited for; matrix products, arithmetic and copies ran while one was open for 1% of the time, Pallas kernels for 0%

commit v1 on v0

v1 whole, which is shorter than its diff:
```python
import jax
import jax.numpy as jnp
from jax import lax
from jax.sharding import Mesh, PartitionSpec as P

logit_scale = 20.0

AXES = ("yh", "x", "zh", "zl", "yl", "core")
SIZES = (4, 4, 4, 2, 2, 2)
PASS_AXES = ("x", "yl", "zl")
CHIP_AXES = ("yh", "zh")
QUERY_AXES = ("yh", "zh", "core")


def exchange(blocks, axes):
    return lax.all_to_all(blocks, axes, 0, 0, tiled=True)


def spread(x, n):
    return lax.optimization_barrier(jnp.broadcast_to(x[None], (n,) + x.shape))


def scores_of(q, p):
    return logit_scale * lax.dot_general(
        q, p, (((1,), (1,)), ((), ())), preferred_element_type=jnp.float32
    )


def lse(x, axis):
    peak = x.max(axis=axis)
    return peak + jnp.log(jnp.exp(x - jnp.expand_dims(peak, axis)).sum(axis=axis))


def local(query, passage, positive):
    rows, embed = query.shape
    n_pass = lax.axis_size(PASS_AXES)
    n_chip = lax.axis_size(CHIP_AXES)
    n_query = lax.axis_size(QUERY_AXES)
    n_p = n_pass * rows
    half = n_chip * rows
    core = lax.axis_index("core")
    swap = [(0, 1), (1, 0)]

    own = exchange(spread(query, n_chip), CHIP_AXES).reshape(half, embed)
    other = lax.ppermute(own, "core", swap)
    pall = exchange(spread(passage, n_pass), PASS_AXES).reshape(n_p, embed)

    slot = jnp.arange(rows, dtype=jnp.int32)
    onehot = (positive[0][:, None] == slot[None, :]).astype(jnp.bfloat16)
    paired_passage = jnp.dot(onehot, passage, preferred_element_type=jnp.float32)
    paired_query = lax.dot_general(
        onehot, query, (((0,), (0,)), ((), ())), preferred_element_type=jnp.float32
    )
    positive_sum = logit_scale * jnp.sum(query.astype(jnp.float32) * paired_passage)

    s0 = scores_of(own, pall)
    s1 = scores_of(other, pall)
    row0, row1 = lse(s0, 1), lse(s1, 1)
    col_peak = jnp.maximum(s0.max(axis=0), s1.max(axis=0))
    col_part = col_peak + jnp.log(
        jnp.exp(s0 - col_peak[None, :]).sum(axis=0) + jnp.exp(s1 - col_peak[None, :]).sum(axis=0)
    )

    col_all = exchange(spread(col_part.reshape(-1, 128), n_pass), PASS_AXES)
    col_lse = lse(col_all.reshape(n_pass, n_p), 0)

    first = jnp.where(core == 0, row0, row1)
    second = jnp.where(core == 0, row1, row0)
    lane = jnp.arange(128)
    extra = jnp.where(lane == 0, jnp.sum(col_lse), 0.0) + jnp.where(lane == 1, positive_sum, 0.0)
    extra = jnp.broadcast_to(extra[None], (8, 128))
    msg = jnp.concatenate([first.reshape(-1, 128), second.reshape(-1, 128), extra], axis=0)
    row_all = exchange(spread(msg, n_query), QUERY_AXES)
    k = half // 128
    row_can = lse(row_all[:, : 2 * k], 0).reshape(2, half)
    row_lse0 = jnp.where(core == 0, row_can[0], row_can[1])
    row_lse1 = jnp.where(core == 0, row_can[1], row_can[0])
    totals = row_all[:, 2 * k].sum(axis=0)
    side = jnp.sum(row_can) - 2.0 * totals[1]
    loss = (lax.psum(side, PASS_AXES) + totals[0]) / (2.0 * n_pass * n_query * rows)

    def weights(s, row_lse):
        return (0.5 * (jnp.exp(s - row_lse[:, None]) + jnp.exp(s - col_lse[None, :]))).astype(
            jnp.bfloat16
        )

    w1 = weights(s1, row_lse1)
    w0 = weights(s0, row_lse0)
    given = jnp.dot(w1, pall, preferred_element_type=jnp.float32).astype(jnp.bfloat16)
    taken = lax.ppermute(given, "core", swap)
    tn = (((0,), (0,)), ((), ()))
    pgrad = lax.dot_general(w0, own, tn, preferred_element_type=jnp.float32) + lax.dot_general(
        w1, other, tn, preferred_element_type=jnp.float32
    )
    pgrad = exchange(pgrad.astype(jnp.bfloat16).reshape(n_pass, rows, embed), PASS_AXES)
    qgrad = jnp.dot(w0, pall, preferred_element_type=jnp.float32) + taken.astype(jnp.float32)
    qgrad = exchange(qgrad.astype(jnp.bfloat16).reshape(n_chip, rows, embed), CHIP_AXES)

    query_sum = qgrad.astype(jnp.float32).sum(axis=0)
    passage_sum = pgrad.astype(jnp.float32).sum(axis=0)
    grad_query = (logit_scale * (query_sum - paired_passage)).astype(jnp.bfloat16)
    grad_passage = (logit_scale * (passage_sum - paired_query)).astype(jnp.bfloat16)
    return (loss, grad_query, grad_passage)


def solution(mesh):
    cut = Mesh(mesh.devices.reshape(SIZES), AXES)
    spec = P(AXES, None)
    return jax.shard_map(
        local,
        mesh=cut,
        in_specs=(spec, spec, spec),
        out_specs=(P(), spec, spec),
        check_vma=False,
    )
```

time: 659 us -> 199 us (0.30)
  the two profiles are of different devices: /device:TPU:1 before, /device:TPU:16 now
where the time goes in v1:
time: 199 us; the launch traced here: 198 us
  blocking collectives  76.4 us (38%)
  waiting for transfers between devices  57.7 us (29%)
  starting transfers between devices  36.8 us (18%)
  matrix products  13.3 us (7%)
  between operations  5.21 us (3%)
  local copies, waits for them, and re-layouts  4.43 us (2%)
  other arithmetic  4.17 us (2%)
    all_to_all x5, waiting for transfers between devices, exchange(): return lax.all_to_all(blocks, axes, 0, 0, tiled=True)  55.1 us
    psum x1, blocking collectives, local(): lax.psum(side, PASS_AXES) + totals[0]  53 us
    all_to_all x5, starting transfers between devices, exchange(): return lax.all_to_all(blocks, axes, 0, 0, tiled=True)  32.9 us
    all_to_all x1, blocking collectives, exchange(): return lax.all_to_all(blocks, axes, 0, 0, tiled=True)  23.4 us
  transfers between devices with their start and end apart: 7, of which 5 were waited for; matrix products, arithmetic and copies ran while one was open for 5% of the time, Pallas kernels for 0%

profile of v1, /device:TPU:16, one launch (start us, length us, event | category | flops | bytes accessed | tf_op | source)
XLA Modules:
  0.0 198.0 jit_solution(14112436553538395940)
XLA Ops:
  0.6 0.0 copy-start.6
  0.6 2.0 %broadcast_in_dim.22 = bf16[16,32,1024]{2,1,0:T(8,128)(2,1)} broadcast(bf16[32,1024]{1,0:T(8,128)(2,1)} %param.3), dimensions={1,2} | broadcast | bytes 1114112 | tf_op jit(solution)/shard_map/broadcast_in_dim | solution.py:20
  2.6 15.9 %all-to-all-start = ((bf16[16,32,1024]{2,1,0:T(8,128)(2,1)}), bf16[16,32,1024]{2,1,0:T(8,128)(2,1)S(1)}, u32[]{:S(2)}, u32[]{:S(2)}) async-start(bf16[16,32,1024]{2,1,0:T(8,128)(2,1)} %broadcast_in_dim.22), calls=%async_computation | async-start | bytes 2097152 | tf_op jit(solution)/shard_map/all_to_all | solution.py:16
  18.5 0.0 copy-done.6
  18.5 1.2 broadcast_in_dim.23
  19.7 29.1 %all-to-all-done = bf16[16,32,1024]{2,1,0:T(8,128)(2,1)S(1)} async-done(((bf16[16,32,1024]{2,1,0:T(8,128)(2,1)}), bf16[16,32,1024]{2,1,0:T(8,128)(2,1)S(1)}, u32[]{:S(2)}, u32[]{:S(2)}) %all-to-all-start) | async-done | bytes 1048608 | tf_op jit(solution)/shard_map/all_to_all | solution.py:16
  48.8 5.1 %all-to-all-start.1 = ((bf16[16,32,1024]{2,1,0:T(8,128)(2,1)}), bf16[16,32,1024]{2,1,0:T(8,128)(2,1)S(1)}, u32[]{:S(2)}, u32[]{:S(2)}) async-start(bf16[16,32,1024]{2,1,0:T(8,128)(2,1)} %broadcast_in_dim.23), calls=%async_computation.1 | async-start | bytes 2097152 | tf_op jit(solution)/shard_map/all_to_all | solution.py:16
  53.9 1.9 collective-permute-start
  55.9 13.2 %all-to-all-done.1 = bf16[16,32,1024]{2,1,0:T(8,128)(2,1)S(1)} async-done(((bf16[16,32,1024]{2,1,0:T(8,128)(2,1)}), bf16[16,32,1024]{2,1,0:T(8,128)(2,1)S(1)}, u32[]{:S(2)}, u32[]{:S(2)}) %all-to-all-start.1) | async-done | bytes 1048608 | tf_op jit(solution)/shard_map/all_to_all | solution.py:16
  69.1 0.8 fusion.11
  69.9 0.0 copy-done.2
  69.9 0.0 copy-start.4
  69.9 0.0 copy-start.7
  70.0 0.0 collective-permute-done
  70.0 2.1 %fusion.10 = (f32[512]{0:T(512)S(1)}, f32[512]{0:T(512)S(1)}, f32[512,512]{1,0:T(8,128)S(1)}) fusion(bf16[512,1024]{1,0:T(8,128)(2,1)} %collective-permute-done, bf16[512,1024]{1,0:T(8,128)(2,1)S(1)} %bitcast.31), kind=kOutput, calls=%fused_computation.42 | convolution fusion | flops 537656320 | bytes 3149824 | tf_op jit(solution)/shard_map/dot_general | solution.py:24
  72.0 0.0 copy-done
  72.0 0.0 copy-start.3
  72.1 1.1 exponential_reduce_fusion.2
  73.2 0.6 broadcast_in_dim.24
  73.8 3.7 %all-to-all-start.2 = ((f32[16,4,128]{2,1,0:T(4,128)}), f32[16,4,128]{2,1,0:T(4,128)S(1)}, u32[]{:S(2)}, u32[]{:S(2)}) async-start(f32[16,4,128]{2,1,0:T(4,128)} %broadcast_in_dim.24), calls=%async_computation.2 | async-start | bytes 65536 | tf_op jit(solution)/shard_map/all_to_all | solution.py:16
  77.5 0.0 copy-done.4
  77.5 0.0 copy-done.7
  77.5 1.5 multiply_reduce_fusion
  79.6 5.0 %all-to-all-done.2 = f32[16,4,128]{2,1,0:T(4,128)S(1)} async-done(((f32[16,4,128]{2,1,0:T(4,128)}), f32[16,4,128]{2,1,0:T(4,128)S(1)}, u32[]{:S(2)}, u32[]{:S(2)}) %all-to-all-start.2) | async-done | bytes 32800 | tf_op jit(solution)/shard_map/all_to_all | solution.py:16
  84.6 0.6 fusion.5
  85.3 0.6 fusion.7
  86.0 23.4 %all_to_all.30 = f32[32,16,128]{2,1,0:T(8,128)S(1)} all-to-all(f32[32,16,128]{2,1,0:T(8,128)S(1)} %broadcast_in_dim.29), channel_id=1, replica_groups=mesh['yh'=4,'x'=4,'zh'=4,'zl'=2,'yl'=2,'core'=2] {'yh','zh','core'}, dimensions={0} | all-to-all | bytes 524288 | tf_op jit(solution)/shard_map/all_to_all | solution.py:16
  109.5 0.6 fusion.12
  110.1 0.0 copy-done.3
  110.1 0.9 fusion.8
  111.0 3.1 %add_convert_fusion = bf16[512,1024]{1,0:T(8,128)(2,1)} fusion(f32[512,1024]{1,0:T(8,128)S(1)} %fusion.8, bf16[512,1024]{1,0:T(8,128)(2,1)} %collective-permute-done, f32[512,512]{1,0:T(8,128)S(1)} %get-tuple-element.26, f32[512]{0:T(512)S(1)} %get-tuple-element.16, f32[512]{0:T(512)S(1)} %get-tuple-element.17), kind=kOutput, calls=%fused_computation.1 | convolution fusion | flops 539230208 | bytes 5246976 | tf_op jit(solution)/shard_map/dot_general | solution.py:92
  114.1 3.7 %all-to-all-start.5 = ((bf16[16,32,1024]{2,1,0:T(8,128)(2,1)}), bf16[16,32,1024]{2,1,0:T(8,128)(2,1)S(1)}, u32[]{:S(2)}, u32[]{:S(2)}) async-start(bf16[16,32,1024]{2,1,0:T(8,128)(2,1)} %bitcast.37), calls=%async_computation.5 | async-start | bytes 2097152 | tf_op jit(solution)/shard_map/all_to_all | solution.py:16
  117.7 0.0 copy-start.1
  117.8 2.2 %convolution_convert_fusion = bf16[512,1024]{1,0:T(8,128)(2,1)S(1)} fusion(bf16[512,1024]{1,0:T(8,128)(2,1)} %bitcast.32, f32[512,512]{1,0:T(8,128)S(1)} %get-tuple-element.26, f32[512]{0:T(512)S(1)} %get-tuple-element.16, f32[512]{0:T(512)S(1)} %get-tuple-element.17), kind=kOutput, calls=%fused_computation.4 | convolution fusion | flops 538705920 | bytes 3149824 | tf_op jit(solution)/shard_map/dot_general | solution.py:89
  119.9 2.0 %collective-permute-start.1 = (bf16[512,1024]{1,0:T(8,128)(2,1)S(1)}, bf16[512,1024]{1,0:T(8,128)(2,1)S(1)}, u32[]{:S(2)}, u32[]{:S(2)}) collective-permute-start(bf16[512,1024]{1,0:T(8,128)(2,1)S(1)} %convolution_convert_fusion), channel_id=1, source_target_pairs={{0,1},{1,0},{2,3},{3,2},{4,5},{5,4},{6,7},{7,6},{8,9},{9,8},{10,11... | collective-permute-start | bytes 3145736 | tf_op jit(solution)/shard_map/ppermute | solution.py:90
  122.0 2.5 %collective-permute-done.1 = bf16[512,1024]{1,0:T(8,128)(2,1)S(1)} collective-permute-done((bf16[512,1024]{1,0:T(8,128)(2,1)S(1)}, bf16[512,1024]{1,0:T(8,128)(2,1)S(1)}, u32[]{:S(2)}, u32[]{:S(2)}) %collective-permute-start.1) | collective-permute-done | bytes 1048608 | tf_op jit(solution)/shard_map/ppermute | solution.py:90
  124.5 0.0 copy-done.1
  124.5 1.9 add_convert_fusion.1
  126.4 7.9 %all-to-all-done.5 = bf16[16,32,1024]{2,1,0:T(8,128)(2,1)S(1)} async-done(((bf16[16,32,1024]{2,1,0:T(8,128)(2,1)}), bf16[16,32,1024]{2,1,0:T(8,128)(2,1)S(1)}, u32[]{:S(2)}, u32[]{:S(2)}) %all-to-all-start.5) | async-done | bytes 1048608 | tf_op jit(solution)/shard_map/all_to_all | solution.py:16
  134.2 4.5 %all-to-all-start.4 = ((bf16[16,32,1024]{2,1,0:T(8,128)(2,1)}), bf16[16,32,1024]{2,1,0:T(8,128)(2,1)S(1)}, u32[]{:S(2)}, u32[]{:S(2)}) async-start(bf16[16,32,1024]{2,1,0:T(8,128)(2,1)} %bitcast.12), calls=%async_computation.4 | async-start | bytes 2097152 | tf_op jit(solution)/shard_map/all_to_all | solution.py:16
  138.8 0.6 fusion.13
  140.6 53.0 %psum.7 = f32[]{:T(128)} all-reduce(f32[]{:T(128)S(6)} %sub.97), channel_id=1, replica_groups=mesh['yh'=4,'x'=4,'zh'=4,'zl'=2,'yl'=2,'core'=2] {'x','yl','zl'}, use_global_device_ids=true, to_apply=%region_16.17 | all-reduce | flops 1 | bytes 8 | tf_op jit(solution)/shard_map/psum | solution.py:80
  195.0 0.2 convert_reduce_fusion
  195.2 0.9 fusion.1
  196.1 0.0 all-to-all-done.4
  196.1 0.2 convert_reduce_fusion.1
  196.3 0.0 copy-done.5
  196.3 0.6 multiply_convert_fusion.2
  (15 shorter events, 0.2 us)
Async XLA Ops:
  0.6 17.9 %copy-start.6 = (bf16[32,1024]{1,0:T(8,128)(2,1)S(1)}, bf16[32,1024]{1,0:T(8,128)(2,1)}, u32[]{:S(2)}) copy-start(bf16[32,1024]{1,0:T(8,128)(2,1)} %param.4) | copy-start | bytes 196612
  2.6 46.2 %all-to-all-start = ((bf16[16,32,1024]{2,1,0:T(8,128)(2,1)}), bf16[16,32,1024]{2,1,0:T(8,128)(2,1)S(1)}, u32[]{:S(2)}, u32[]{:S(2)}) async-start(bf16[16,32,1024]{2,1,0:T(8,128)(2,1)} %broadcast_in_dim.22), calls=%async_computation | async-start | bytes 2097152 | tf_op jit(solution)/shard_map/all_to_all | solution.py:16
  48.8 21.1 %copy-start.2 = (bf16[16,32,1024]{2,1,0:T(8,128)(2,1)}, bf16[16,32,1024]{2,1,0:T(8,128)(2,1)S(1)}, u32[]{:S(2)}) copy-start(bf16[16,32,1024]{2,1,0:T(8,128)(2,1)S(1)} %all-to-all-done) | copy-start | bytes 3145732
  48.8 20.3 %all-to-all-start.1 = ((bf16[16,32,1024]{2,1,0:T(8,128)(2,1)}), bf16[16,32,1024]{2,1,0:T(8,128)(2,1)S(1)}, u32[]{:S(2)}, u32[]{:S(2)}) async-start(bf16[16,32,1024]{2,1,0:T(8,128)(2,1)} %broadcast_in_dim.23), calls=%async_computation.1 | async-start | bytes 2097152 | tf_op jit(solution)/shard_map/all_to_all | solution.py:16
  53.9 16.0 %collective-permute-start = (bf16[512,1024]{1,0:T(8,128)(2,1)S(1)}, bf16[512,1024]{1,0:T(8,128)(2,1)}, u32[]{:S(2)}, u32[]{:S(2)}) collective-permute-start(bf16[512,1024]{1,0:T(8,128)(2,1)S(1)} %bitcast.34), channel_id=1, source_target_pairs={{0,1},{1,0},{2,3},{3,2},{4,5},{5,4},{6,7},{7,6},{8,9},{9,8},{10,11... | collective-permute-start | bytes 3145736 | tf_op jit(solution)/shard_map/ppermute | solution.py:45
  69.1 2.9 %copy-start = (bf16[16,32,1024]{2,1,0:T(8,128)(2,1)}, bf16[16,32,1024]{2,1,0:T(8,128)(2,1)S(1)}, u32[]{:S(2)}) copy-start(bf16[16,32,1024]{2,1,0:T(8,128)(2,1)S(1)} %all-to-all-done.1) | copy-start | bytes 3145732
  69.9 7.6 %copy-start.4 = (bf16[32,1024]{1,0:T(8,128)(2,1)S(1)}, bf16[32,1024]{1,0:T(8,128)(2,1)}, u32[]{:S(2)}) copy-start(bf16[32,1024]{1,0:T(8,128)(2,1)} %param.3) | copy-start | bytes 196612
  69.9 7.6 %copy-start.7 = (s32[1,32]{1,0:T(1,128)S(1)}, s32[1,32]{1,0:T(1,128)}, u32[]{:S(2)}) copy-start(s32[1,32]{1,0:T(1,128)} %param.5) | copy-start | bytes 388
  72.0 38.1 %copy-start.3 = (bf16[16,32,1024]{2,1,0:T(8,128)(2,1)S(1)}, bf16[16,32,1024]{2,1,0:T(8,128)(2,1)}, u32[]{:S(2)}) copy-start(bf16[16,32,1024]{2,1,0:T(8,128)(2,1)} %copy-done.2) | copy-start | bytes 3145732
  73.8 10.8 %all-to-all-start.2 = ((f32[16,4,128]{2,1,0:T(4,128)}), f32[16,4,128]{2,1,0:T(4,128)S(1)}, u32[]{:S(2)}, u32[]{:S(2)}) async-start(f32[16,4,128]{2,1,0:T(4,128)} %broadcast_in_dim.24), calls=%async_computation.2 | async-start | bytes 65536 | tf_op jit(solution)/shard_map/all_to_all | solution.py:16
  114.1 20.1 %all-to-all-start.5 = ((bf16[16,32,1024]{2,1,0:T(8,128)(2,1)}), bf16[16,32,1024]{2,1,0:T(8,128)(2,1)S(1)}, u32[]{:S(2)}, u32[]{:S(2)}) async-start(bf16[16,32,1024]{2,1,0:T(8,128)(2,1)} %bitcast.37), calls=%async_computation.5 | async-start | bytes 2097152 | tf_op jit(solution)/shard_map/all_to_all | solution.py:16
  117.7 6.7 %copy-start.1 = (bf16[16,32,1024]{2,1,0:T(8,128)(2,1)S(1)}, bf16[16,32,1024]{2,1,0:T(8,128)(2,1)}, u32[]{:S(2)}) copy-start(bf16[16,32,1024]{2,1,0:T(8,128)(2,1)} %copy-done) | copy-start | bytes 3145732
  119.9 4.6 %collective-permute-start.1 = (bf16[512,1024]{1,0:T(8,128)(2,1)S(1)}, bf16[512,1024]{1,0:T(8,128)(2,1)S(1)}, u32[]{:S(2)}, u32[]{:S(2)}) collective-permute-start(bf16[512,1024]{1,0:T(8,128)(2,1)S(1)} %convolution_convert_fusion), channel_id=1, source_target_pairs={{0,1},{1,0},{2,3},{3,2},{4,5},{5,4},{6,7},{7,6},{8,9},{9,8},{10,11... | collective-permute-start | bytes 3145736 | tf_op jit(solution)/shard_map/ppermute | solution.py:90
  134.2 62.0 %copy-start.5 = (f32[32,1024]{1,0:T(8,128)S(1)}, f32[32,1024]{1,0:T(8,128)}, u32[]{:S(2)}) copy-start(f32[32,1024]{1,0:T(8,128)} %get-tuple-element.24) | copy-start | bytes 393220
  134.2 61.8 %all-to-all-start.4 = ((bf16[16,32,1024]{2,1,0:T(8,128)(2,1)}), bf16[16,32,1024]{2,1,0:T(8,128)(2,1)S(1)}, u32[]{:S(2)}, u32[]{:S(2)}) async-start(bf16[16,32,1024]{2,1,0:T(8,128)(2,1)} %bitcast.12), calls=%async_computation.4 | async-start | bytes 2097152 | tf_op jit(solution)/shard_map/all_to_all | solution.py:16
